TPU v7x, 512 devices: a whole 4x8x8 slice. The times are simulated.
512 devices in a mesh: region: 16 (over y, core), var: 32 (over z, x).
Axes of the slice: x: 4, y: 8, z: 8, core: 2. Of those that a mesh axis runs over, the one named last changes fastest.
Arguments:
- state: float32 [262144, 768], P(('region', 'var')), may hold values from -6 to 6
- taper: bfloat16 [4, 262144, 384], P(None, ('region', 'var')), may hold values from 0.19921875 to 1
- block_mask: int32 [4, 2048, 3], P(None, ('region', 'var')), may hold values 0 or 1
- anom_fly: float32 [16, 384, 768], P('region', 'var'), may hold values from -6 to 6
- incr_fly: float32 [16, 384, 768], P('region', 'var'), may hold values from -6 to 6
- anom_new: float32 [3, 384, 768], P(None, 'var'), may hold values from -6 to 6
- incr_new: float32 [3, 384, 768], P(None, 'var'), may hold values from -6 to 6
Outputs:
- updated: float32 [262144, 768], P(('region', 'var'))
All inputs are finite; a program needn't handle non-finite values. No bound on the sum of `block_mask` on one device may be relied on, other than what follows from the above.
Results may differ from a plain program's by a relative error of at most 0.0003.
Values sent between devices are 32-bit elements; how exact they have to be, the bound alone decides.
No kernel may reach another device: no remote copies, remote signals or barrier semaphores. Data moves between devices by JAX's collectives and lax.ppermute only.
A program may use at most 64 MiB of HBM per device.

v0:
```python
import jax
import jax.numpy as jnp
from jax import lax
from jax.sharding import PartitionSpec as P

MEMBERS = 768
BLOCK = 128
TICKS = 4


def shifted(block, axis, distance):
    devices = range(lax.axis_size(axis))
    route = [(i - distance, i) for i in devices if i - distance in devices]
    return lax.ppermute(block, axis, route)


def localizer(taper_now, block_flags):
    row_blocks, obs_blocks = block_flags.shape
    expanded = jnp.broadcast_to(
        block_flags[:, None, :, None], (row_blocks, BLOCK, obs_blocks, BLOCK)
    )
    expanded = expanded.reshape(row_blocks * BLOCK, obs_blocks * BLOCK).astype(jnp.float32)
    return taper_now.astype(jnp.float32) * expanded


def assimilate(state_rows, taper_now, block_flags, batch_pair):
    localize = localizer(taper_now, block_flags)
    gathered = lax.all_gather(batch_pair, "var", axis=1, tiled=True)
    covar = lax.dot_general(
        state_rows,
        gathered[0],
        (((1,), (1,)), ((), ())),
        precision=lax.Precision.HIGHEST,
        preferred_element_type=jnp.float32,
    )
    weights = localize * covar / (MEMBERS - 1)
    increment = jnp.dot(
        weights, gathered[1], precision=lax.Precision.HIGHEST, preferred_element_type=jnp.float32
    )
    return state_rows + increment


def on_device(state, taper, block_mask, anom_fly, incr_fly, anom_new, incr_new):
    region_id = lax.axis_index("region")
    in_flight = jnp.stack([anom_fly[0], incr_fly[0]])
    entering = jnp.stack([anom_new, incr_new], 1)
    state_rows = state
    batch_pair = in_flight
    for tick_num in range(TICKS):
        if tick_num > 0:
            arrived = shifted(batch_pair, "region", 1)
            batch_pair = jnp.where(region_id == 0, entering[tick_num - 1], arrived)
        state_rows = assimilate(state_rows, taper[tick_num], block_mask[tick_num], batch_pair)
    return state_rows


def solution(mesh):
    in_specs = (
        P(("region", "var"), None),
        P(None, ("region", "var"), None),
        P(None, ("region", "var"), None),
        P("region", "var", None),
        P("region", "var", None),
        P(None, "var", None),
        P(None, "var", None),
    )
    out_specs = P(("region", "var"), None)
    return jax.shard_map(
        on_device, mesh=mesh, in_specs=in_specs, out_specs=out_specs, check_vma=False
    )
```

profile of v0, /device:TPU:8, one launch (start us, length us, event | category | flops | bytes accessed | tf_op | source)
XLA Modules:
  0.0 368.7 jit_solution(4278995919764913455)
XLA Ops:
  6.5 1.6 pad_maximum_fusion.1
  8.2 1.9 collective-permute-start
  10.1 1.0 stack.13
  12.1 2.0 collective-permute-done
  14.9 1.9 collective-permute-start.1
  16.8 4.5 %collective-permute-done.1 = f32[2,12,768]{2,0,1:T(2,128)S(1)} collective-permute-done((f32[2,12,768]{2,0,1:T(2,128)}, f32[2,12,768]{2,0,1:T(2,128)S(1)}, u32[]{:S(2)}, u32[]{:S(2)}) %collective-permute-start.1) | collective-permute-done | bytes 73760 | tf_op jit(solution)/shard_map/ppermute | solution.py:14
  22.1 1.9 collective-permute-start.2
  24.0 4.0 %collective-permute-done.2 = f32[2,12,768]{2,0,1:T(2,128)S(1)} collective-permute-done((f32[2,12,768]{2,0,1:T(2,128)}, f32[2,12,768]{2,0,1:T(2,128)S(1)}, u32[]{:S(2)}, u32[]{:S(2)}) %collective-permute-start.2) | collective-permute-done | bytes 73760 | tf_op jit(solution)/shard_map/ppermute | solution.py:14
  31.5 67.4 %all-gather.5.cloned.1.call-done = f32[2,384,768]{2,0,1:T(2,128)} async-done(((f32[2,12,768]{2,0,1:T(2,128)}), f32[2,384,768]{2,0,1:T(2,128)}) %all-gather.5.cloned.1.call-update) | async-done | bytes 2359312 | tf_op jit(solution)/shard_map/all_gather | solution.py:28
  99.0 4.5 %fusion.28 = (f32[1,384,768]{2,0,1:T(1,128)S(1)}, f32[1,384,768]{2,0,1:T(1,128)S(1)}) fusion(f32[2,384,768]{2,0,1:T(2,128)} %all-gather.5.cloned.1.call-done), kind=kLoop, calls=%fused_computation.52 | loop fusion | bytes 4718592 | tf_op jit(solution)/shard_map/slice | solution.py:38
  103.7 2.1 fusion.1
  105.8 2.9 convolution_add_fusion.3
  108.7 74.4 %all-gather.7.cloned.1.call-done = f32[2,384,768]{2,0,1:T(2,128)} async-done(((f32[2,12,768]{2,0,1:T(2,128)}), f32[2,384,768]{2,0,1:T(2,128)}) %all-gather.7.cloned.1.call-update) | async-done | bytes 2359312 | tf_op jit(solution)/shard_map/all_gather | solution.py:28
  183.1 4.4 %fusion.27 = (f32[1,384,768]{2,0,1:T(1,128)S(1)}, f32[1,384,768]{2,0,1:T(1,128)S(1)}) fusion(f32[2,384,768]{2,0,1:T(2,128)} %all-gather.7.cloned.1.call-done), kind=kLoop, calls=%fused_computation.51 | loop fusion | bytes 4718592 | tf_op jit(solution)/shard_map/slice | solution.py:38
  187.7 2.3 fusion.2
  190.1 2.8 convolution_add_fusion.2
  192.9 74.4 %all-gather.9.cloned.1.call-done = f32[2,384,768]{2,0,1:T(2,128)} async-done(((f32[2,12,768]{2,0,1:T(2,128)}), f32[2,384,768]{2,0,1:T(2,128)}) %all-gather.9.cloned.1.call-update) | async-done | bytes 2359312 | tf_op jit(solution)/shard_map/all_gather | solution.py:28
  267.3 4.4 %fusion.26 = (f32[1,384,768]{2,0,1:T(1,128)S(1)}, f32[1,384,768]{2,0,1:T(1,128)S(1)}) fusion(f32[2,384,768]{2,0,1:T(2,128)} %all-gather.9.cloned.1.call-done), kind=kLoop, calls=%fused_computation.50 | loop fusion | bytes 4718592 | tf_op jit(solution)/shard_map/slice | solution.py:38
  271.9 2.1 fusion.3
  274.0 2.8 convolution_add_fusion.1
  276.8 74.5 %all-gather.11.cloned.1.call-done = f32[2,384,768]{2,0,1:T(2,128)} async-done(((f32[2,12,768]{2,0,1:T(2,128)}), f32[2,384,768]{2,0,1:T(2,128)}) %all-gather.11.cloned.1.call-update) | async-done | bytes 2359312 | tf_op jit(solution)/shard_map/all_gather | solution.py:28
  351.3 4.6 %fusion.25 = (f32[1,384,768]{2,0,1:T(1,128)S(1)}, f32[1,384,768]{2,0,1:T(1,128)S(1)}) fusion(f32[2,384,768]{2,0,1:T(2,128)} %all-gather.11.cloned.1.call-done), kind=kLoop, calls=%fused_computation.49 | loop fusion | bytes 4718592 | tf_op jit(solution)/shard_map/slice | solution.py:38
  356.1 2.1 fusion.4
  358.3 4.0 %convolution_add_fusion = f32[512,768]{1,0:T(8,128)} fusion(f32[512,768]{1,0:T(8,128)S(1)} %convolution_add_fusion.1, f32[512,384]{0,1:T(8,128)S(1)} %fusion.4, f32[1,384,768]{2,0,1:T(1,128)S(1)} %get-tuple-element.5), kind=kOutput, calls=%fused_computation | convolution fusion | flops 1812332544 | bytes 5111808 | tf_op jit(solution)/shard_map/dot_general | solution.py:37
  (42 shorter events, 6.8 us)
Async XLA Ops:
  6.5 22.2 %copy-start.1 = (bf16[4,512,384]{2,1,0:T(8,128)(2,1)S(1)}, bf16[4,512,384]{2,1,0:T(8,128)(2,1)}, u32[]{:S(2)}) copy-start(bf16[4,512,384]{2,1,0:T(8,128)(2,1)} %param.8) | copy-start | bytes 4718596
  6.5 92.5 %all-gather.5.cloned.1.call-start = ((), (), s32[]{:S(2)}) async-start(), calls=%async_computation | async-start | bytes 2433024 | tf_op jit(solution)/shard_map/all_gather | solution.py:28
  8.2 175.0 %all-gather.7.cloned.1.call-start = ((), (), s32[]{:S(2)}) async-start(), calls=%async_computation.1 | async-start | bytes 2433024 | tf_op jit(solution)/shard_map/all_gather | solution.py:28
  8.2 5.9 %collective-permute-start = (f32[2,12,768]{2,0,1:T(2,128)}, f32[2,12,768]{2,0,1:T(2,128)S(1)}, u32[]{:S(2)}, u32[]{:S(2)}) collective-permute-start(f32[2,12,768]{2,0,1:T(2,128)} %pad_maximum_fusion.1), channel_id=1, source_target_pairs={{0,32},{32,64},{64,96},{96,128},{128,160},{160,192},{192,224},{224... | collective-permute-start | bytes 221192 | tf_op jit(solution)/shard_map/ppermute | solution.py:14
  14.8 252.5 %all-gather.9.cloned.1.call-start = ((), (), s32[]{:S(2)}) async-start(), calls=%async_computation.2 | async-start | bytes 2433024 | tf_op jit(solution)/shard_map/all_gather | solution.py:28
  14.9 6.4 %collective-permute-start.1 = (f32[2,12,768]{2,0,1:T(2,128)}, f32[2,12,768]{2,0,1:T(2,128)S(1)}, u32[]{:S(2)}, u32[]{:S(2)}) collective-permute-start(f32[2,12,768]{2,0,1:T(2,128)} %bitcast_select_fusion.1), channel_id=1, source_target_pairs={{0,32},{32,64},{64,96},{96,128},{128,160},{160,192},{192,224},{224... | collective-permute-start | bytes 221192 | tf_op jit(solution)/shard_map/ppermute | solution.py:14
  22.0 329.3 %all-gather.11.cloned.1.call-start = ((), (), s32[]{:S(2)}) async-start(), calls=%async_computation.3 | async-start | bytes 2433024 | tf_op jit(solution)/shard_map/all_gather | solution.py:28
  22.1 5.9 %collective-permute-start.2 = (f32[2,12,768]{2,0,1:T(2,128)}, f32[2,12,768]{2,0,1:T(2,128)S(1)}, u32[]{:S(2)}, u32[]{:S(2)}) collective-permute-start(f32[2,12,768]{2,0,1:T(2,128)} %bitcast_select_fusion), channel_id=1, source_target_pairs={{0,32},{32,64},{64,96},{96,128},{128,160},{160,192},{192,224},{224... | collective-permute-start | bytes 221192 | tf_op jit(solution)/shard_map/ppermute | solution.py:14
  28.7 0.7 copy-start.3
  99.0 4.7 %copy-start = (f32[512,768]{1,0:T(8,128)S(1)}, f32[512,768]{1,0:T(8,128)}, u32[]{:S(2)}) copy-start(f32[512,768]{1,0:T(8,128)} %param.7) | copy-start | bytes 4718596
  192.9 79.0 %copy-start.2 = (bf16[1,512,384]{1,2,0:T(8,128)(2,1)S(1)}, bf16[1,512,384]{1,2,0:T(8,128)(2,1)}, u32[]{:S(2)}) copy-start(bf16[1,512,384]{1,2,0:T(8,128)(2,1)} %copy.77) | copy-start | bytes 1179652
Sparse Core Ops, SparseCore 0:
  10.5 88.4 all-gather.4
  102.2 80.9 all-gather.6
  186.3 80.9 all-gather.8
  270.3 80.9 all-gather.10
where the time goes:
time: 369 us
  waiting for transfers between devices  301 us (82%)
  local copies, waits for them, and re-layouts  23.4 us (6%)
  matrix products  21.1 us (6%)
  between operations  13.3 us (4%)
  starting transfers between devices  5.89 us (2%)
  other arithmetic  3.75 us (1%)
    all_gather x4, waiting for transfers between devices, assimilate(): gathered = lax.all_gather(batch_pair, 'var', axis=1, tiled=True)  291 us
    slice x4, local copies, waits for them, and re-layouts, assimilate(): gathered[1]  17.9 us
    dot_general x4, matrix products, assimilate(): jnp.dot(weights, gathered[1], precision=lax.Precision.HIGHEST, preferred_...  12.4 us
    ppermute x3, waiting for transfers between devices, shifted(): return lax.ppermute(block, axis, route)  10.4 us
    dot_general x4, matrix products, assimilate(): lax.dot_general(state_rows, gathered[0], (((1,), (1,)), ((), ())), precis...  8.67 us
  transfers between devices with their start and end apart: 7, of which 7 were waited for; matrix products, arithmetic and copies ran while one was open for 10% of the time, Pallas kernels for 0%

commit v1 on v0

--- a/solution.py
+++ b/solution.py
@@ -2,6 +2,7 @@
 import jax.numpy as jnp
 from jax import lax
 from jax.sharding import PartitionSpec as P
+from jax.lax import all_to_all, psum
 
 MEMBERS = 768
 BLOCK = 128
@@ -25,7 +26,15 @@
 
 def assimilate(state_rows, taper_now, block_flags, batch_pair):
     localize = localizer(taper_now, block_flags)
-    gathered = lax.all_gather(batch_pair, "var", axis=1, tiled=True)
+    gathered = jnp.concatenate(
+        all_to_all(
+            jnp.stack([batch_pair for _ in range(psum(1, "var"))], 0),
+            "var",
+            split_axis=0,
+            concat_axis=0,
+        ),
+        axis=1,
+    )
     covar = lax.dot_general(
         state_rows,
         gathered[0],

time: 369 us -> 299 us (0.81)
  the two profiles are of different devices: /device:TPU:8 before, /device:TPU:26 now
where the time goes in v1:
time: 299 us; the launch traced here: 294 us
  waiting for transfers between devices  150 us (50%)
  local copies, waits for them, and re-layouts  75.5 us (25%)
  starting transfers between devices  40 us (13%)
  matrix products  26.4 us (9%)
    all_to_all x4, waiting for transfers between devices, assimilate(): all_to_all(jnp.stack([batch_pair for _ in range(psum(1, 'var'))], 0), 'va...  141 us
    slice x4, local copies, waits for them, and re-layouts, assimilate(): gathered[1]  37.4 us
    all_to_all x4, starting transfers between devices, assimilate(): all_to_all(jnp.stack([batch_pair for _ in range(psum(1, 'var'))], 0), 'va...  34.2 us
    dot_general x4, matrix products, assimilate(): lax.dot_general(state_rows, gathered[0], (((1,), (1,)), ((), ())), precis...  14.1 us
    dot_general x4, matrix products, assimilate(): jnp.dot(weights, gathered[1], precision=lax.Precision.HIGHEST, preferred_...  12.3 us
    squeeze x4, local copies, waits for them, and re-layouts, assimilate(): gathered[0]  10.8 us
    another operation x4, local copies, waits for them, and re-layouts, assimilate(): jnp.stack([batch_pair for _ in range(psum(1, 'var'))], 0)  9.04 us
    ppermute x3, waiting for transfers between devices, shifted(): return lax.ppermute(block, axis, route)  8.15 us
  transfers between devices with their start and end apart: 7, of which 6 were waited for; matrix products, arithmetic and copies ran while one was open for 24% of the time, Pallas kernels for 0%

profile of v1, /device:TPU:26, one launch (start us, length us, event | category | flops | bytes accessed | tf_op | source)
XLA Modules:
  0.0 293.7 jit_solution(13391390276890241191)
XLA Ops:
  3.6 13.6 %all-to-all-start = ((f32[32,2,12,768]{3,1,2,0:T(2,128)}), f32[32,2,12,768]{3,1,2,0:T(2,128)S(1)}, u32[]{:S(2)}, u32[]{:S(2)}) async-start(f32[32,2,12,768]{3,1,2,0:T(2,128)} %stack.17), calls=%async_computation | async-start | bytes 4718592 | tf_op jit(solution)/shard_map/all_to_all | solution.py:30
  19.2 4.0 %collective-permute-done = f32[2,12,768]{2,1,0:T(8,128)S(1)} collective-permute-done((f32[2,12,768]{2,1,0:T(8,128)S(1)}, f32[2,12,768]{2,1,0:T(8,128)S(1)}, u32[]{:S(2)}, u32[]{:S(2)}) %collective-permute-start) | collective-permute-done | bytes 73760 | tf_op jit(solution)/shard_map/ppermute | solution.py:15
  23.3 48.6 %all-to-all-done = f32[32,2,12,768]{3,1,2,0:T(2,128)S(1)} async-done(((f32[32,2,12,768]{3,1,2,0:T(2,128)}), f32[32,2,12,768]{3,1,2,0:T(2,128)S(1)}, u32[]{:S(2)}, u32[]{:S(2)}) %all-to-all-start) | async-done | bytes 2359328 | tf_op jit(solution)/shard_map/all_to_all | solution.py:30
  73.9 6.5 %all-to-all-start.1 = ((f32[32,2,12,768]{3,1,2,0:T(2,128)}), f32[32,2,12,768]{3,1,2,0:T(2,128)}, u32[]{:S(2)}, u32[]{:S(2)}) async-start(f32[32,2,12,768]{3,1,2,0:T(2,128)} %stack.21), calls=%async_computation.1 | async-start | bytes 4718592 | tf_op jit(solution)/shard_map/all_to_all | solution.py:30
  82.4 4.0 %collective-permute-done.1 = f32[2,12,768]{2,1,0:T(8,128)S(1)} collective-permute-done((f32[2,12,768]{2,1,0:T(8,128)S(1)}, f32[2,12,768]{2,1,0:T(8,128)S(1)}, u32[]{:S(2)}, u32[]{:S(2)}) %collective-permute-start.1) | collective-permute-done | bytes 73760 | tf_op jit(solution)/shard_map/ppermute | solution.py:15
  88.0 46.9 %all-to-all-done.1 = f32[32,2,12,768]{3,1,2,0:T(2,128)} async-done(((f32[32,2,12,768]{3,1,2,0:T(2,128)}), f32[32,2,12,768]{3,1,2,0:T(2,128)}, u32[]{:S(2)}, u32[]{:S(2)}) %all-to-all-start.1) | async-done | bytes 2359328 | tf_op jit(solution)/shard_map/all_to_all | solution.py:30
  136.9 7.1 %all-to-all-start.2 = ((f32[32,2,12,768]{3,1,2,0:T(2,128)}), f32[32,2,12,768]{3,1,2,0:T(2,128)}, u32[]{:S(2)}, u32[]{:S(2)}) async-start(f32[32,2,12,768]{3,1,2,0:T(2,128)} %stack.22), calls=%async_computation.2 | async-start | bytes 4718592 | tf_op jit(solution)/shard_map/all_to_all | solution.py:30
  151.9 45.9 %all-to-all-done.2 = f32[32,2,12,768]{3,1,2,0:T(2,128)} async-done(((f32[32,2,12,768]{3,1,2,0:T(2,128)}), f32[32,2,12,768]{3,1,2,0:T(2,128)}, u32[]{:S(2)}, u32[]{:S(2)}) %all-to-all-start.2) | async-done | bytes 2359328 | tf_op jit(solution)/shard_map/all_to_all | solution.py:30
  197.9 3.0 %stack.23 = f32[32,2,12,768]{3,1,2,0:T(2,128)} broadcast(f32[2,12,768]{2,0,1:T(2,128)} %copy.76), dimensions={1,2,3} | broadcast | bytes 2433024 | tf_op jit(solution)/shard_map/stack | solution.py:31
  200.8 7.0 %all-to-all-start.3 = ((f32[32,2,12,768]{3,1,2,0:T(2,128)}), f32[32,2,12,768]{3,1,2,0:T(2,128)}, u32[]{:S(2)}, u32[]{:S(2)}) async-start(f32[32,2,12,768]{3,1,2,0:T(2,128)} %stack.23), calls=%async_computation.3 | async-start | bytes 4718592 | tf_op jit(solution)/shard_map/all_to_all | solution.py:30
  212.8 7.4 %slice_reduce_fusion.6 = (f32[32,12,768]{2,1,0:T(8,128)}, f32[32,12,768]{2,1,0:T(8,128)}) fusion(f32[2,32,12,768]{3,0,2,1:T(2,128)S(1)} %bitcast.96), kind=kLoop, calls=%fused_computation.19 | loop fusion | bytes 4718592 | tf_op jit(solution)/shard_map/slice | solution.py:47
  220.2 2.7 squeeze.37
  224.9 3.5 %fusion.1 = f32[512,384]{0,1:T(8,128)S(1)} fusion(f32[384,768]{1,0:T(8,128)} %squeeze.37, f32[512,768]{1,0:T(8,128)S(1)} %copy-done, f32[48,8,4,128]{3,2,1,0:T(4,128)S(1)} %bitcast.97, bf16[1,512,384]{1,2,0:T(8,128)(2,1)} %copy.89), kind=kOutput, calls=%fused_computation.9 | convolution fusion | flops 1812725760 | bytes 4718592 | tf_op jit(solution)/shard_map/dot_general | solution.py:38
  228.4 2.8 convolution_add_fusion.3
  231.2 10.0 %slice_reduce_fusion.4 = (f32[32,12,768]{2,1,0:T(8,128)S(1)}, f32[32,12,768]{2,1,0:T(8,128)}) fusion(f32[2,32,12,768]{3,0,2,1:T(2,128)} %bitcast.9), kind=kLoop, calls=%fused_computation.17 | loop fusion | bytes 4718592 | tf_op jit(solution)/shard_map/slice | solution.py:47
  241.2 2.9 squeeze.40
  245.4 3.6 %fusion.2 = f32[512,384]{0,1:T(8,128)S(1)} fusion(f32[512,768]{1,0:T(8,128)S(1)} %convolution_add_fusion.3, f32[384,768]{1,0:T(8,128)} %squeeze.40, f32[48,8,4,128]{3,2,1,0:T(4,128)S(1)} %bitcast.98, bf16[1,512,384]{1,2,0:T(8,128)(2,1)} %copy.91), kind=kOutput, calls=%fused_computation.10 | convolution fusion | flops 1812725760 | bytes 4718592 | tf_op jit(solution)/shard_map/dot_general | solution.py:38
  249.0 2.8 convolution_add_fusion.2
  251.8 10.0 %slice_reduce_fusion.2 = (f32[32,12,768]{2,1,0:T(8,128)S(1)}, f32[32,12,768]{2,1,0:T(8,128)}) fusion(f32[2,32,12,768]{3,0,2,1:T(2,128)} %bitcast.13), kind=kLoop, calls=%fused_computation.15 | loop fusion | bytes 4718592 | tf_op jit(solution)/shard_map/slice | solution.py:47
  265.7 3.6 %fusion.3 = f32[512,384]{0,1:T(8,128)S(1)} fusion(f32[512,768]{1,0:T(8,128)S(1)} %convolution_add_fusion.2, f32[384,768]{1,0:T(8,128)} %squeeze.43, f32[48,8,4,128]{3,2,1,0:T(4,128)S(1)} %bitcast.99, bf16[1,512,384]{1,2,0:T(8,128)(2,1)} %copy.94), kind=kOutput, calls=%fused_computation.11 | convolution fusion | flops 1812725760 | bytes 4718592 | tf_op jit(solution)/shard_map/dot_general | solution.py:38
  269.3 2.8 convolution_add_fusion.1
  272.1 10.0 %slice_reduce_fusion = (f32[32,12,768]{2,1,0:T(8,128)S(1)}, f32[32,12,768]{2,1,0:T(8,128)}) fusion(f32[2,32,12,768]{3,0,2,1:T(2,128)} %bitcast.17), kind=kLoop, calls=%fused_computation.13 | loop fusion | bytes 4718592 | tf_op jit(solution)/shard_map/slice | solution.py:47
  286.1 3.5 %fusion.4 = f32[512,384]{0,1:T(8,128)S(1)} fusion(f32[512,768]{1,0:T(8,128)S(1)} %convolution_add_fusion.1, f32[384,768]{1,0:T(8,128)} %squeeze.46, f32[48,8,4,128]{3,2,1,0:T(4,128)S(1)} %bitcast.100, bf16[1,512,384]{1,2,0:T(8,128)(2,1)S(1)} %copy.97), kind=kOutput, calls=%fused_computation.12 | convolution fusion | flops 1812725760 | bytes 4718592 | tf_op jit(solution)/shard_map/dot_general | solution.py:38
  289.5 3.9 %convolution_add_fusion = f32[512,768]{1,0:T(8,128)} fusion(f32[512,768]{1,0:T(8,128)S(1)} %convolution_add_fusion.1, f32[512,384]{0,1:T(8,128)S(1)} %fusion.4, f32[384,768]{1,0:T(8,128)S(1)} %copy-done.4), kind=kOutput, calls=%fused_computation | convolution fusion | flops 1812332544 | bytes 5111808 | tf_op jit(solution)/shard_map/dot_general | solution.py:46
  (63 shorter events, 37.1 us)
Async XLA Ops:
  3.6 19.5 %copy-start.6 = (f32[3,12,768]{2,1,0:T(8,128)S(1)}, f32[3,12,768]{2,1,0:T(8,128)}, u32[]{:S(2)}) copy-start(f32[3,12,768]{2,1,0:T(8,128)} %param.12) | copy-start | bytes 331780
  3.6 19.5 %copy-start.7 = (f32[3,12,768]{2,1,0:T(8,128)S(1)}, f32[3,12,768]{2,1,0:T(8,128)}, u32[]{:S(2)}) copy-start(f32[3,12,768]{2,1,0:T(8,128)} %param.13) | copy-start | bytes 331780
  3.6 68.2 %all-to-all-start = ((f32[32,2,12,768]{3,1,2,0:T(2,128)}), f32[32,2,12,768]{3,1,2,0:T(2,128)S(1)}, u32[]{:S(2)}, u32[]{:S(2)}) async-start(f32[32,2,12,768]{3,1,2,0:T(2,128)} %stack.17), calls=%async_computation | async-start | bytes 4718592 | tf_op jit(solution)/shard_map/all_to_all | solution.py:30
  17.2 5.9 %collective-permute-start = (f32[2,12,768]{2,1,0:T(8,128)S(1)}, f32[2,12,768]{2,1,0:T(8,128)S(1)}, u32[]{:S(2)}, u32[]{:S(2)}) collective-permute-start(f32[2,12,768]{2,1,0:T(8,128)S(1)} %copy_dynamic-update-slice_fusion), channel_id=1, source_target_pairs={{0,32},{32,64},{64,96},{96,128},{128,160},{160,192},{192,224},{224... | collective-permute-start | bytes 221192 | tf_op jit(solution)/shard_map/ppermute | solution.py:15
  73.9 61.0 %all-to-all-start.1 = ((f32[32,2,12,768]{3,1,2,0:T(2,128)}), f32[32,2,12,768]{3,1,2,0:T(2,128)}, u32[]{:S(2)}, u32[]{:S(2)}) async-start(f32[32,2,12,768]{3,1,2,0:T(2,128)} %stack.21), calls=%async_computation.1 | async-start | bytes 4718592 | tf_op jit(solution)/shard_map/all_to_all | solution.py:30
  80.5 5.9 %collective-permute-start.1 = (f32[2,12,768]{2,1,0:T(8,128)S(1)}, f32[2,12,768]{2,1,0:T(8,128)S(1)}, u32[]{:S(2)}, u32[]{:S(2)}) collective-permute-start(f32[2,12,768]{2,1,0:T(8,128)S(1)} %fusion.10), channel_id=1, source_target_pairs={{0,32},{32,64},{64,96},{96,128},{128,160},{160,192},{192,224},{224... | collective-permute-start | bytes 221192 | tf_op jit(solution)/shard_map/ppermute | solution.py:15
  136.9 60.9 %all-to-all-start.2 = ((f32[32,2,12,768]{3,1,2,0:T(2,128)}), f32[32,2,12,768]{3,1,2,0:T(2,128)}, u32[]{:S(2)}, u32[]{:S(2)}) async-start(f32[32,2,12,768]{3,1,2,0:T(2,128)} %stack.22), calls=%async_computation.2 | async-start | bytes 4718592 | tf_op jit(solution)/shard_map/all_to_all | solution.py:30
  144.0 6.3 %collective-permute-start.2 = (f32[2,12,768]{2,1,0:T(8,128)}, f32[2,12,768]{2,1,0:T(8,128)}, u32[]{:S(2)}, u32[]{:S(2)}) collective-permute-start(f32[2,12,768]{2,1,0:T(8,128)} %fusion.7), channel_id=1, source_target_pairs={{0,32},{32,64},{64,96},{96,128},{128,160},{160,192},{192,224},{224... | collective-permute-start | bytes 221192 | tf_op jit(solution)/shard_map/ppermute | solution.py:15
  200.8 71.3 %all-to-all-start.3 = ((f32[32,2,12,768]{3,1,2,0:T(2,128)}), f32[32,2,12,768]{3,1,2,0:T(2,128)}, u32[]{:S(2)}, u32[]{:S(2)}) async-start(f32[32,2,12,768]{3,1,2,0:T(2,128)} %stack.23), calls=%async_computation.3 | async-start | bytes 4718592 | tf_op jit(solution)/shard_map/all_to_all | solution.py:30
  209.4 2.2 copy-start.8
  220.2 2.8 copy-start.1
  223.0 1.8 copy-start
  224.8 3.6 %copy-start.5 = (f32[384,768]{1,0:T(8,128)S(1)}, f32[384,768]{1,0:T(8,128)}, u32[]{:S(2)}) copy-start(f32[384,768]{1,0:T(8,128)} %squeeze.38) | copy-start | bytes 3538948
  245.4 3.6 %copy-start.2 = (f32[384,768]{1,0:T(8,128)S(1)}, f32[384,768]{1,0:T(8,128)}, u32[]{:S(2)}) copy-start(f32[384,768]{1,0:T(8,128)} %squeeze.41) | copy-start | bytes 3538948
  265.7 3.6 %copy-start.3 = (f32[384,768]{1,0:T(8,128)S(1)}, f32[384,768]{1,0:T(8,128)}, u32[]{:S(2)}) copy-start(f32[384,768]{1,0:T(8,128)} %squeeze.44) | copy-start | bytes 3538948
  286.0 3.5 %copy-start.4 = (f32[384,768]{1,0:T(8,128)S(1)}, f32[384,768]{1,0:T(8,128)}, u32[]{:S(2)}) copy-start(f32[384,768]{1,0:T(8,128)} %squeeze.47) | copy-start | bytes 3538948
